TPU v7x, 32 devices: a whole 2x2x4 slice. The times are simulated.
32 devices in a mesh: seq: 4 (over y, x), dp: 4 (over z), enc: 2 (over core).
Axes of the slice: x: 2, y: 2, z: 4, core: 2. Of those that a mesh axis runs over, the one named last changes fastest.
Arguments:
- lm_grad: bfloat16 [4, 4, 192, 1152], P('dp', 'enc', 'seq'), may hold values from -6 to 6
- image_tokens: int32 [4, 4, 4], P('dp'), may hold values from 1 to 15, as said below
- image_offset: int32 [4, 4, 4], P('dp'), may hold values from 0 to 47, as said below
- image_owner: int32 [4, 4, 4], P('dp'), may hold values from 0 to 3, as said below
- mlp_input: bfloat16 [4, 4, 240, 1152], P('dp', None, 'seq'), may hold values from -36 to 36
- layer_output: bfloat16 [4, 4, 240, 1152], P('dp', 'enc', 'seq'), may hold values from -36 to 36
- pre_gain: float32 [1152], replicated, may hold values from 0.5 to 1.5
- pre_bias: float32 [1152], replicated, may hold values from -3 to 3
- fc1_weight: bfloat16 [1152, 4304], P(None, 'enc'), may hold values from -0.1875 to 0.1875
- fc1_bias: float32 [4304], P('enc'), may hold values from -3 to 3
- fc2_weight: bfloat16 [4304, 1152], P('enc'), may hold values from -0.09375 to 0.09375
- post_gain: float32 [1152], replicated, may hold values from 0.5 to 1.5
- post_bias: float32 [1152], replicated, may hold values from -3 to 3
- merge_gain: float32 [1152], replicated, may hold values from 0.5 to 1.5
Outputs:
- act_grad: bfloat16 [4, 4, 240, 1152], P('dp', 'enc', 'seq')
- norm_grads: float32 [6, 1152], replicated
- fc1_bias_grad: float32 [4304], replicated
Inputs may be any that keep to these rules, and one draw needn't show every extreme that they name: `image_tokens`: the 4 images of one LM shard have token counts that sum to 48, and one of them has 15. `image_offset`: the images of one LM shard lie back to back over its 48 rows, in some order; each entry is an image's first row in its shard. Images are placed round-robin by their index j in a shard: image_owner[r, q, j] = (q + image_owner[r, 0, j]) mod 4, with the 4 values image_owner[r, 0, j] different. So each encoder chip owns exactly 4 images of its replica, the visual tokens owned by one chip number at most 60, and some chip owns exactly 60.
All inputs are finite; a program needn't handle non-finite values.
Results may differ from a plain program's by a relative error of at most 0.005.
Values may be sent and summed in bfloat16 or wider, within the bound.
A program may use at most 64 MiB of HBM per device.

v0:
```python
import math

import jax
import jax.numpy as jnp
from jax import lax
from jax.experimental import pallas as pl
from jax.experimental.pallas import tpu as pltpu
from jax.sharding import PartitionSpec as P

MOST_LEN = 15
WINDOW = 16
SUBLANES = 8
HEAD_VMEM = 24 * 1024 * 1024
EPSILON = 1e-06
SLOPE_K = math.sqrt(2.0 / math.pi)
CUBIC = 0.044715
F32 = jnp.float32
BF16 = jnp.bfloat16
MESH_ID = pl.DeviceIdType.MESH


def gelu_slope(pre_act):
    inner_arg = SLOPE_K * (pre_act + CUBIC * pre_act * pre_act * pre_act)
    tangent = jnp.tanh(inner_arg)
    return 0.5 * (1.0 + tangent) + 0.5 * pre_act * (1.0 - tangent * tangent) * SLOPE_K * (
        1.0 + 3.0 * CUBIC * pre_act * pre_act
    )


def row_mean(values):
    return jnp.mean(values, axis=-1, keepdims=True)


def norm_parts(values):
    centred = values - row_mean(values)
    scale = lax.rsqrt(row_mean(centred * centred) + EPSILON)
    return centred * scale, scale


def norm_pull(normal, scale, cotangent):
    return scale * (cotangent - row_mean(cotangent) - normal * row_mean(cotangent * normal))


def greet(peers):
    barrier = pltpu.get_barrier_semaphore()
    for peer in peers:
        pl.semaphore_signal(barrier, inc=1, device_id=peer, device_id_type=MESH_ID)
    return lambda: pl.semaphore_wait(barrier, len(peers))


def others(axis, count):
    me = lax.axis_index(axis)
    return [{axis: lax.rem(me + step, count)} for step in range(1, count)]


def remote(src, dst, send_sem, recv_sem, peer):
    copy = pltpu.make_async_remote_copy(
        src_ref=src,
        dst_ref=dst,
        send_sem=send_sem,
        recv_sem=recv_sem,
        device_id=peer,
        device_id_type=MESH_ID,
    )
    copy.start()
    return copy


def head_kernel(
    shards,
    tokens_ref,
    offsets_ref,
    owners_ref,
    grad_ref,
    layer_ref,
    input_ref,
    pre_gain_ref,
    pre_bias_ref,
    post_gain_ref,
    post_bias_ref,
    merge_ref,
    all_ref,
    res_ref,
    normed_ref,
    sums_ref,
    send_buf,
    recv_buf,
    swap_out,
    swap_in,
    seq_send,
    seq_recv,
    enc_send,
    enc_recv,
):
    me = lax.axis_index("seq")
    core = lax.axis_index("enc")
    partner = {"enc": 1 - core}
    own, rows_dev, width = grad_ref.shape
    slots = layer_ref.shape[1]
    peers = others("seq", shards)
    settle = greet([partner] + peers)
    images = tokens_ref.shape[1]
    places = shards * WINDOW
    place = lax.broadcasted_iota(jnp.int32, (places, rows_dev), 0)
    chip, step = place // WINDOW, place % WINDOW
    source = jnp.full((places, rows_dev), -1, jnp.int32)
    for image in range(images):
        taken = (chip == owners_ref[me, image]) & (step < tokens_ref[me, image])
        source = jnp.where(taken, offsets_ref[me, image] + step, source)
    row = lax.broadcasted_iota(jnp.int32, (places, rows_dev), 1)
    pack = jnp.where(row == source, 1.0, 0.0).astype(BF16)
    for patch in range(own):
        packed = jnp.dot(pack, grad_ref[patch], preferred_element_type=F32)
        send_buf[:, patch] = packed.astype(BF16).reshape(shards, WINDOW, width)
    settle()
    copies = []
    for step, peer in enumerate(peers):
        copies.append(
            remote(
                send_buf.at[peer["seq"]],
                recv_buf.at[me],
                seq_send.at[step],
                seq_recv.at[step],
                peer,
            )
        )
    recv_buf[me] = send_buf[me]
    pre_gain = pre_gain_ref[...].reshape(1, -1)
    pre_bias = pre_bias_ref[...].reshape(1, -1)
    normed_ref[...] = jnp.zeros_like(normed_ref)
    for patch in range(input_ref.shape[0]):
        normal, _ = norm_parts(input_ref[patch].astype(F32))
        normed_ref[patch, 0:slots, :] = (normal * pre_gain + pre_bias).astype(BF16)
    post_gain = post_gain_ref[...].reshape(1, -1)
    post_bias = post_bias_ref[...].reshape(1, -1)
    merge_gain = merge_ref[...].reshape(1, -1)
    swap_out[...] = jnp.zeros_like(swap_out)
    place = lax.broadcasted_iota(jnp.int32, (slots, places), 1)
    chip, step = place // WINDOW, place % WINDOW
    target = jnp.full((slots, places), -1, jnp.int32)
    first = jnp.int32(0)
    for shard in range(shards):
        count = jnp.int32(0)
        for image in range(images):
            count += jnp.where(owners_ref[shard, image] == me, tokens_ref[shard, image], 0)
        target = jnp.where((chip == shard) & (step < count), first + step, target)
        first += count
    slot = lax.broadcasted_iota(jnp.int32, (slots, places), 0)
    unpack = jnp.where(slot == target, 1.0, 0.0).astype(BF16)
    for copy in copies:
        copy.wait()
    swaps = []
    totals = None
    for patch in range(own):
        landed = recv_buf[:, patch].reshape(shards * WINDOW, width)
        incoming = jnp.dot(unpack, landed, preferred_element_type=F32)
        normal, scale = norm_parts(layer_ref[patch].astype(F32))
        affine = normal * post_gain + post_bias
        rms = lax.rsqrt(row_mean(affine * affine) + EPSILON)
        unit = affine * rms
        unit_grad = incoming * merge_gain
        affine_grad = rms * (unit_grad - unit * row_mean(unit_grad * unit))
        res = norm_pull(normal, scale, affine_grad * post_gain)
        res_ref[patch] = res
        swap_out[patch, 0:slots, :] = res.astype(BF16)
        parts = [
            jnp.sum(term, axis=0, keepdims=True)
            for term in (incoming * unit, affine_grad * normal, affine_grad, res)
        ]
        totals = parts if totals is None else [a + b for a, b in zip(totals, parts)]
        swaps.append(
            remote(
                swap_out.at[patch],
                swap_in.at[patch],
                enc_send.at[patch],
                enc_recv.at[patch],
                partner,
            )
        )
        all_ref[core * own + patch] = swap_out[patch]
    sums_ref[...] = jnp.zeros_like(sums_ref)
    for index, total in enumerate(totals):
        sums_ref[index : index + 1, :] = total
    for patch in range(own):
        swaps[patch].wait()
        all_ref[(1 - core) * own + patch] = swap_in[patch]


def tail_kernel(
    shards,
    replicas,
    grad_scale,
    product_ref,
    input_ref,
    pre_gain_ref,
    res_ref,
    sums_ref,
    units_ref,
    act_ref,
    norm_ref,
    unit_ref,
    swap_out,
    swap_in,
    normals,
    halves,
    half_in,
    seq_buf,
    dp_buf,
    last_buf,
    enc_send,
    enc_recv,
    seq_send,
    seq_recv,
    dp_send,
    dp_recv,
):
    me = lax.axis_index("seq")
    replica = lax.axis_index("dp")
    core = lax.axis_index("enc")
    other = 1 - core
    partner = {"enc": other}
    own = act_ref.shape[0]
    slots = act_ref.shape[1]
    seq_peers = others("seq", shards)
    dp_peers = others("dp", replicas)
    settle = greet([partner] + seq_peers + dp_peers)
    halves[...] = jnp.zeros_like(halves)
    width = act_ref.shape[2]
    hidden = units_ref.shape[1]
    spans = [(at, min(width, hidden - at)) for at in range(0, hidden, width)]
    halves[0, 0:1, :] = sums_ref[0:1, :]
    halves[0, 1:2, :] = sums_ref[1:2, :]
    halves[0, 2:3, :] = sums_ref[2:3, :]
    halves[1, 0:1, :] = sums_ref[3:4, :]
    for index, (at, size) in enumerate(spans):
        halves[core, 3 + index : 4 + index, 0:size] = units_ref[:, at : at + size]
    for patch in range(own):
        swap_out[patch] = product_ref[other * own + patch].astype(BF16)
    settle()
    swaps = [
        remote(
            swap_out.at[patch],
            swap_in.at[patch],
            enc_send.at[patch],
            enc_recv.at[patch],
            partner,
        )
        for patch in range(own)
    ]
    pre_gain = pre_gain_ref[...].reshape(1, -1)
    scales = []
    for patch in range(own):
        normal, scale = norm_parts(input_ref[core * own + patch].astype(F32))
        normals[patch] = normal
        scales.append(scale)
    gain_grad = None
    for patch in range(own):
        swaps[patch].wait()
        upstream = product_ref[core * own + patch, 0:slots, :] + swap_in[patch, 0:slots, :].astype(F32)
        parts = [
            jnp.sum(upstream * normals[patch], axis=0, keepdims=True),
            jnp.sum(upstream, axis=0, keepdims=True),
        ]
        gain_grad = parts if gain_grad is None else [a + b for a, b in zip(gain_grad, parts)]
    halves[1, 1:2, :] = gain_grad[0]
    halves[1, 2:3, :] = gain_grad[1]

    def finish(patch):
        upstream = product_ref[core * own + patch, 0:slots, :] + swap_in[patch, 0:slots, :].astype(F32)
        act = res_ref[patch] + norm_pull(normals[patch], scales[patch], upstream * pre_gain)
        act_ref[patch] = act.astype(BF16)

    half_copy = remote(halves.at[other], half_in, enc_send.at[own], enc_recv.at[own], partner)
    finish(0)
    half_copy.wait()
    seq_buf[me] = halves[core] + half_in[...]
    copies = [
        remote(seq_buf.at[me], seq_buf.at[me], seq_send.at[step], seq_recv.at[step], peer)
        for step, peer in enumerate(seq_peers)
    ]
    for patch in range(1, own):
        finish(patch)
    for copy in copies:
        copy.wait()
    total = seq_buf[0]
    for index in range(1, shards):
        total = total + seq_buf[index]
    dp_buf[replica] = total
    copies = [
        remote(dp_buf.at[replica], dp_buf.at[replica], dp_send.at[step], dp_recv.at[step], peer)
        for step, peer in enumerate(dp_peers)
    ]
    for copy in copies:
        copy.wait()
    total = dp_buf[0]
    for index in range(1, replicas):
        total = total + dp_buf[index]
    last_buf[core] = total * grad_scale
    remote(
        last_buf.at[core], last_buf.at[core], enc_send.at[own + 1], enc_recv.at[own + 1], partner
    ).wait()
    for half in range(2):
        norm_ref[3 * half : 3 * half + 3, :] = last_buf[half, 0:3, :]
        for index, (at, size) in enumerate(spans):
            unit_ref[half : half + 1, at : at + size] = last_buf[half, 3 + index : 4 + index, 0:size]


def round_up(value, step):
    return (value + step - 1) // step * step


def body(
    lm_grad,
    image_tokens,
    image_offset,
    image_owner,
    mlp_input,
    layer_output,
    pre_gain,
    pre_bias,
    fc1_weight,
    fc1_bias,
    fc2_weight,
    post_gain,
    post_bias,
    merge_gain,
):
    shards = lax.axis_size("seq")
    replicas = lax.axis_size("dp")
    cores = lax.axis_size("enc")
    grad_rows = lm_grad[0]
    input_rows = mlp_input[0]
    layer_rows = layer_output[0]
    own, rows_dev, width = grad_rows.shape
    group, slots, _ = input_rows.shape
    padded = round_up(slots, WINDOW)

    vmem = pl.BlockSpec(memory_space=pltpu.VMEM)
    dma = pltpu.SemaphoreType.DMA

    def head_call(*refs):
        head_kernel(shards, *refs)

    all_res, res_grad, normed, sums = pl.pallas_call(
        head_call,
        out_shape=(
            jax.ShapeDtypeStruct((group, padded, width), BF16),
            jax.ShapeDtypeStruct((own, slots, width), F32),
            jax.ShapeDtypeStruct((group, padded, width), BF16),
            jax.ShapeDtypeStruct((SUBLANES, width), F32),
        ),
        in_specs=[pl.BlockSpec(memory_space=pltpu.SMEM)] * 3 + [vmem] * 8,
        out_specs=(vmem,) * 4,
        scratch_shapes=[
            pltpu.VMEM((shards, own, WINDOW, width), BF16),
            pltpu.VMEM((shards, own, WINDOW, width), BF16),
            pltpu.VMEM((own, padded, width), BF16),
            pltpu.VMEM((own, padded, width), BF16),
            dma((shards - 1,)),
            dma((shards - 1,)),
            dma((own,)),
            dma((own,)),
        ],
        compiler_params=pltpu.CompilerParams(
            collective_id=0, has_side_effects=True, vmem_limit_bytes=HEAD_VMEM
        ),
        cost_estimate=pl.CostEstimate(flops=4_000_000_000, bytes_accessed=24_000_000, transcendentals=0),
        name="head",
    )(
        image_tokens[0],
        image_offset[0],
        image_owner[0],
        grad_rows,
        layer_rows,
        input_rows,
        pre_gain,
        pre_bias,
        post_gain,
        post_bias,
        merge_gain,
    )

    pre_act = (
        jnp.dot(normed.reshape(-1, width), fc1_weight, preferred_element_type=F32) + fc1_bias
    )
    down_back = lax.dot_general(
        all_res.reshape(-1, width),
        fc2_weight,
        (((1,), (1,)), ((), ())),
        preferred_element_type=F32,
    )
    hidden_grad = down_back * gelu_slope(pre_act)
    units = jnp.sum(hidden_grad, axis=0, keepdims=True)
    hidden_units = fc1_bias.shape[0]
    product = lax.dot_general(
        hidden_grad.astype(BF16),
        fc1_weight,
        (((1,), (1,)), ((), ())),
        preferred_element_type=F32,
    ).reshape(group, padded, width)
    unit_rows = round_up(hidden_units, width) // width

    grad_scale = 1.0 / math.sqrt(group * rows_dev * shards * replicas)
    sum_rows = round_up(3 + unit_rows, SUBLANES)

    def tail_call(*refs):
        tail_kernel(shards, replicas, grad_scale, *refs)

    act_grad, norm_grads, unit_grads = pl.pallas_call(
        tail_call,
        out_shape=(
            jax.ShapeDtypeStruct((own, slots, width), BF16),
            jax.ShapeDtypeStruct((6, width), F32),
            jax.ShapeDtypeStruct((cores, hidden_units), F32),
        ),
        in_specs=[vmem] * 6,
        out_specs=(vmem,) * 3,
        scratch_shapes=[
            pltpu.VMEM((own, padded, width), BF16),
            pltpu.VMEM((own, padded, width), BF16),
            pltpu.VMEM((own, slots, width), F32),
            pltpu.VMEM((cores, sum_rows, width), F32),
            pltpu.VMEM((sum_rows, width), F32),
            pltpu.VMEM((shards, sum_rows, width), F32),
            pltpu.VMEM((replicas, sum_rows, width), F32),
            pltpu.VMEM((cores, sum_rows, width), F32),
            dma((own + 2,)),
            dma((own + 2,)),
            dma((shards - 1,)),
            dma((shards - 1,)),
            dma((replicas - 1,)),
            dma((replicas - 1,)),
        ],
        compiler_params=pltpu.CompilerParams(collective_id=1, has_side_effects=True),
        name="tail",
    )(product, input_rows, pre_gain, res_grad, sums, units)
    return (act_grad[None], norm_grads, unit_grads.reshape(-1))


def solution(mesh):
    in_specs = (
        P("dp", "enc", "seq", None),
        P("dp", None, None),
        P("dp", None, None),
        P("dp", None, None),
        P("dp", None, "seq", None),
        P("dp", "enc", "seq", None),
        P(),
        P(),
        P(None, "enc"),
        P("enc"),
        P("enc", None),
        P(),
        P(),
        P(),
    )
    out_specs = (P("dp", "enc", "seq", None), P(), P())
    return jax.shard_map(body, mesh=mesh, in_specs=in_specs, out_specs=out_specs, check_vma=False)
```

profile of v0, /device:TPU:0, one launch (start us, length us, event | category | flops | bytes accessed | tf_op | source)
XLA Modules:
  0.0 51.3 jit_solution(17867264203184265957)
XLA Ops:
  0.6 1.0 %copy.23 = bf16[1,2,60,1152]{3,2,1,0:T(8,128)(2,1)S(1)} copy(bf16[1,2,60,1152]{3,1,2,0:T(2,128)(2,1)} %param.19) | data formatting | bytes 552960 | tf_op args[5]
  1.6 1.1 %copy.22 = bf16[1,4,60,1152]{3,2,1,0:T(8,128)(2,1)S(1)} copy(bf16[1,4,60,1152]{3,1,2,0:T(4,128)(2,1)} %param.18) | data formatting | bytes 1105920 | tf_op args[4]
  2.7 0.0 copy-start
  2.7 0.0 copy-start.3
  2.8 0.7 %copy-done.3 = f32[1152]{0:T(1024)S(1)} copy-done((f32[1152]{0:T(1024)S(1)}, f32[1152]{0:T(1024)}, u32[]{:S(2)}) %copy-start.3) | copy-done | bytes 4632
  3.5 0.0 copy-start.4
  3.5 0.9 %copy-done.4 = bf16[1,2,48,1152]{3,2,1,0:T(8,128)(2,1)S(1)} copy-done((bf16[1,2,48,1152]{3,2,1,0:T(8,128)(2,1)S(1)}, bf16[1,2,48,1152]{3,2,1,0:T(8,128)(2,1)}, u32[]{:S(2)}) %copy-start.4) | copy-done | bytes 221208
  4.4 0.0 copy-start.5
  4.4 0.7 %copy-done.5 = f32[1152]{0:T(1024)S(1)} copy-done((f32[1152]{0:T(1024)S(1)}, f32[1152]{0:T(1024)}, u32[]{:S(2)}) %copy-start.5) | copy-done | bytes 4632
  5.1 0.0 copy-start.6
  5.1 0.7 %copy-done.6 = f32[1152]{0:T(1024)S(1)} copy-done((f32[1152]{0:T(1024)S(1)}, f32[1152]{0:T(1024)}, u32[]{:S(2)}) %copy-start.6) | copy-done | bytes 4632
  5.8 0.0 copy-start.7
  5.8 0.7 %copy-done.7 = f32[1152]{0:T(1024)S(1)} copy-done((f32[1152]{0:T(1024)S(1)}, f32[1152]{0:T(1024)}, u32[]{:S(2)}) %copy-start.7) | copy-done | bytes 4632
  6.5 0.0 copy-start.8
  6.5 0.7 %copy-done.8 = f32[1152]{0:T(1024)S(1)} copy-done((f32[1152]{0:T(1024)S(1)}, f32[1152]{0:T(1024)}, u32[]{:S(2)}) %copy-start.8) | copy-done | bytes 4632
  7.2 0.0 copy-start.9
  7.2 0.7 %copy-done.9 = s32[1,4,4]{2,1,0:T(4,128)S(1)} copy-done((s32[1,4,4]{2,1,0:T(4,128)S(1)}, s32[1,4,4]{2,1,0:T(4,128)}, u32[]{:S(2)}) %copy-start.9) | copy-done | bytes 88
  7.9 0.0 copy-start.10
  7.9 0.7 %copy-done.10 = s32[1,4,4]{2,1,0:T(4,128)S(1)} copy-done((s32[1,4,4]{2,1,0:T(4,128)S(1)}, s32[1,4,4]{2,1,0:T(4,128)}, u32[]{:S(2)}) %copy-start.10) | copy-done | bytes 88
  8.6 0.0 copy-start.11
  8.6 0.7 %copy-done.11 = s32[1,4,4]{2,1,0:T(4,128)S(1)} copy-done((s32[1,4,4]{2,1,0:T(4,128)S(1)}, s32[1,4,4]{2,1,0:T(4,128)}, u32[]{:S(2)}) %copy-start.11) | copy-done | bytes 88
  9.2 0.0 copy-start.13
  9.2 0.0 copy-start.14
  9.2 11.0 %head.1 = (bf16[4,64,1152]{2,1,0:T(8,128)(2,1)S(1)}, f32[2,60,1152]{2,1,0:T(8,128)S(1)}, bf16[4,64,1152]{2,1,0:T(8,128)(2,1)S(1)}, f32[8,1152]{1,0:T(8,128)S(1)}) custom-call(s32[4,4]{1,0:T(4,128)S(1)} %bitcast.24, s32[4,4]{1,0:T(4,128)S(1)} %bitcast.25, s32[4,4]{1,0:T(4,128)S(1)} %bitcast.26, bf16[2,48,1152]{2,1,0:T(8,128)(2,1)S(1)} %bitcast.23, ...), custom_call_target="tpu_custom_call" | custom-call | flops 4000000000 | bytes 24000000 | tf_op jit(solution)/shard_map/head/pallas_call | solution.py:344
  20.3 0.0 copy-done
  20.3 0.0 copy-start.1
  20.3 0.0 copy-start.2
  20.3 0.0 copy-done.13
  20.3 0.0 copy-done.14
  20.3 0.0 copy-start.12
  20.4 1.8 %convolution_add_fusion = f32[256,2152]{0,1:T(8,128)S(1)} fusion(bf16[256,1152]{1,0:T(8,128)(2,1)S(1)} %bitcast.28, bf16[1152,2152]{0,1:T(8,128)(2,1)S(1)} %copy-done.13, f32[2152]{0:T(1024)S(1)} %copy-done.14), kind=kOutput, calls=%fused_computation.1 | convolution fusion | flops 1269852160 | bytes 7760288 | tf_op jit(solution)/shard_map/dot_general | solution.py:384
  22.1 0.0 copy-done.1
  22.1 0.0 copy-done.2
  22.2 0.8 %copy-done.12 = bf16[2152,1152]{1,0:T(8,128)(2,1)S(1)} copy-done((bf16[2152,1152]{1,0:T(8,128)(2,1)S(1)}, bf16[2152,1152]{1,0:T(8,128)(2,1)}, u32[]{:S(2)}) %copy-start.12) | copy-done | bytes 4958232
  23.0 2.8 %fusion.7 = (f32[2152]{0:T(1024)S(1)}, bf16[256,2152]{0,1:T(8,128)(2,1)S(1)}) fusion(f32[256,2152]{0,1:T(8,128)S(1)} %convolution_add_fusion, bf16[256,1152]{1,0:T(8,128)(2,1)S(1)} %bitcast.27, bf16[2152,1152]{1,0:T(8,128)(2,1)S(1)} %copy-done.12), kind=kOutput, calls=%fused_computation.13 | convolution fusion | flops 1280317312 | bytes 8862112 | tf_op jit(solution)/shard_map/dot_general | solution.py:386
  25.7 0.6 %broadcast_in_dim.7.refs_5_ = f32[1,2152]{1,0:T(1,128)} reshape(f32[2152]{0:T(1024)S(1)} %get-tuple-element.20) | data formatting | bytes 17216 | tf_op jit(solution)/shard_map/broadcast_in_dim | solution.py:393
  26.3 2.8 %fusion.5 = f32[256,1152]{1,0:T(8,128)} fusion(bf16[1152,2152]{0,1:T(8,128)(2,1)S(1)} %copy-done.13, bf16[256,2152]{0,1:T(8,128)(2,1)S(1)} %get-tuple-element.21), kind=kOutput, calls=%fused_computation.9 | convolution fusion | flops 1269301248 | bytes 7239680 | tf_op jit(solution)/shard_map/dot_general | solution.py:395
  29.1 17.5 %tail.1 = (bf16[2,60,1152]{2,1,0:T(8,128)(2,1)}, f32[6,1152]{1,0:T(8,128)}, f32[2,2152]{1,0:T(2,128)}) custom-call(f32[4,64,1152]{2,1,0:T(8,128)} %bitcast.29, bf16[4,60,1152]{2,1,0:T(8,128)(2,1)} %bitcast.21, f32[1152]{0:T(1024)} %refs_2_.1, f32[2,60,1152]{2,1,0:T(8,128)} %copy-done.1, f32[8,1152]{1,0:T(8,128)} %copy-done.2, f32[1,2152]{1,0:T(1,128)} %broadcast_in_dim.7.refs_5_), custom_call_target="tpu_custom_call" | custom-call | tf_op jit(solution)/shard_map/tail/pallas_call | solution.py:409
  46.6 2.0 %copy.19 = bf16[1,2,60,1152]{3,1,2,0:T(2,128)(2,1)} copy(bf16[1,2,60,1152]{3,2,1,0:T(8,128)(2,1)} %bitcast.30) | data formatting | bytes 552960
  48.5 1.4 %reshape.22 = f32[4304]{0:T(1024)} reshape(f32[2,2152]{1,0:T(2,128)} %get-tuple-element.16) | data formatting | bytes 34432 | tf_op jit(solution)/shard_map/reshape | solution.py:437
  49.9 1.4 %copy.25 = f32[6,1152]{1,0:T(8,128)} copy(f32[6,1152]{1,0:T(8,128)} %get-tuple-element.28) | data formatting | bytes 55296
Async XLA Ops:
  2.7 17.6 %copy-start = (bf16[1,4,60,1152]{3,2,1,0:T(8,128)(2,1)}, bf16[1,4,60,1152]{3,2,1,0:T(8,128)(2,1)S(1)}, u32[]{:S(2)}) copy-start(bf16[1,4,60,1152]{3,2,1,0:T(8,128)(2,1)S(1)} %copy.22) | copy-start | bytes 1658884
  2.7 0.7 %copy-start.3 = (f32[1152]{0:T(1024)S(1)}, f32[1152]{0:T(1024)}, u32[]{:S(2)}) copy-start(f32[1152]{0:T(1024)} %refs_2_.1) | copy-start | bytes 13828
  3.5 0.9 %copy-start.4 = (bf16[1,2,48,1152]{3,2,1,0:T(8,128)(2,1)S(1)}, bf16[1,2,48,1152]{3,2,1,0:T(8,128)(2,1)}, u32[]{:S(2)}) copy-start(bf16[1,2,48,1152]{3,2,1,0:T(8,128)(2,1)} %param.14) | copy-start | bytes 663556
  4.4 0.7 %copy-start.5 = (f32[1152]{0:T(1024)S(1)}, f32[1152]{0:T(1024)}, u32[]{:S(2)}) copy-start(f32[1152]{0:T(1024)} %refs_7_.1) | copy-start | bytes 13828
  5.1 0.7 %copy-start.6 = (f32[1152]{0:T(1024)S(1)}, f32[1152]{0:T(1024)}, u32[]{:S(2)}) copy-start(f32[1152]{0:T(1024)} %refs_8_.1) | copy-start | bytes 13828
  5.8 0.7 %copy-start.7 = (f32[1152]{0:T(1024)S(1)}, f32[1152]{0:T(1024)}, u32[]{:S(2)}) copy-start(f32[1152]{0:T(1024)} %refs_9_.1) | copy-start | bytes 13828
  6.5 0.7 %copy-start.8 = (f32[1152]{0:T(1024)S(1)}, f32[1152]{0:T(1024)}, u32[]{:S(2)}) copy-start(f32[1152]{0:T(1024)} %refs_10_.1) | copy-start | bytes 13828
  7.2 0.7 %copy-start.9 = (s32[1,4,4]{2,1,0:T(4,128)S(1)}, s32[1,4,4]{2,1,0:T(4,128)}, u32[]{:S(2)}) copy-start(s32[1,4,4]{2,1,0:T(4,128)} %param.15) | copy-start | bytes 196
  7.9 0.7 %copy-start.10 = (s32[1,4,4]{2,1,0:T(4,128)S(1)}, s32[1,4,4]{2,1,0:T(4,128)}, u32[]{:S(2)}) copy-start(s32[1,4,4]{2,1,0:T(4,128)} %param.16) | copy-start | bytes 196
  8.6 0.7 %copy-start.11 = (s32[1,4,4]{2,1,0:T(4,128)S(1)}, s32[1,4,4]{2,1,0:T(4,128)}, u32[]{:S(2)}) copy-start(s32[1,4,4]{2,1,0:T(4,128)} %param.17) | copy-start | bytes 196
  9.2 11.1 %copy-start.13 = (bf16[1152,2152]{0,1:T(8,128)(2,1)S(1)}, bf16[1152,2152]{0,1:T(8,128)(2,1)}, u32[]{:S(2)}) copy-start(bf16[1152,2152]{0,1:T(8,128)(2,1)} %param.22) | copy-start | bytes 14874628
  9.2 11.1 %copy-start.14 = (f32[2152]{0:T(1024)S(1)}, f32[2152]{0:T(1024)}, u32[]{:S(2)}) copy-start(f32[2152]{0:T(1024)} %param.23) | copy-start | bytes 25828
  20.3 1.8 %copy-start.1 = (f32[2,60,1152]{2,1,0:T(8,128)}, f32[2,60,1152]{2,1,0:T(8,128)S(1)}, u32[]{:S(2)}) copy-start(f32[2,60,1152]{2,1,0:T(8,128)S(1)} %get-tuple-element.12.refs_3_) | copy-start | bytes 1658884
  20.3 1.8 %copy-start.2 = (f32[8,1152]{1,0:T(8,128)}, f32[8,1152]{1,0:T(8,128)S(1)}, u32[]{:S(2)}) copy-start(f32[8,1152]{1,0:T(8,128)S(1)} %get-tuple-element.13.refs_4_) | copy-start | bytes 110596
  20.3 2.6 %copy-start.12 = (bf16[2152,1152]{1,0:T(8,128)(2,1)S(1)}, bf16[2152,1152]{1,0:T(8,128)(2,1)}, u32[]{:S(2)}) copy-start(bf16[2152,1152]{1,0:T(8,128)(2,1)} %param.24) | copy-start | bytes 14874628
where the time goes:
time: 52.1 us; the launch traced here: 51.3 us
  Pallas kernels  28.5 us (55%)
  local copies, waits for them, and re-layouts  14.8 us (28%)
  matrix products  7.32 us (14%)
  between operations  0.75 us (1%)
    pallas_call x1, Pallas kernels, body(): pl.pallas_call(tail_call, out_shape=(jax.ShapeDtypeStruct((own, slots, wi...  17.5 us
    unnamed x34, local copies, waits for them, and re-layouts  12.7 us
    pallas_call x1, Pallas kernels, body(): pl.pallas_call(head_call, out_shape=(jax.ShapeDtypeStruct((group, padded,...  11 us
    dot_general x1, matrix products, body(): lax.dot_general(hidden_grad.astype(BF16), fc1_weight, (((1,), (1,)), ((),...  2.78 us
    dot_general x1, matrix products, body(): lax.dot_general(all_res.reshape(-1, width), fc2_weight, (((1,), (1,)), ((...  2.77 us
    dot_general x1, matrix products, body(): jnp.dot(normed.reshape(-1, width), fc1_weight, preferred_element_type=F32)  1.77 us
    reshape x1, local copies, waits for them, and re-layouts, body(): return (act_grad[None], norm_grads, unit_grads.reshape(-1))  1.41 us

commit v1 on v0

v1 whole, which is shorter than its diff:
```python
import math

import jax
import jax.numpy as jnp
from jax import lax
from jax.experimental import pallas as pl
from jax.experimental.pallas import tpu as pltpu
from jax.sharding import PartitionSpec as P

WINDOW = 16
SUB = 8
LANES = 128
CHUNK = 512
PIECES = 3
EPSILON = 1e-06
SLOPE_K = math.sqrt(2.0 / math.pi)
CUBIC = 0.044715
F32 = jnp.float32
BF16 = jnp.bfloat16
MESH_ID = pl.DeviceIdType.MESH
NT = (((1,), (1,)), ((), ()))


def gelu_slope(pre_act):
    square = pre_act * pre_act
    tangent = jnp.tanh(pre_act * (SLOPE_K + (SLOPE_K * CUBIC) * square))
    half = 0.5 + 0.5 * tangent
    return half + half * (1.0 - tangent) * pre_act * (SLOPE_K + (3.0 * SLOPE_K * CUBIC) * square)


def row_mean(values):
    return jnp.mean(values, axis=-1, keepdims=True)


def norm_parts(values):
    centred = values - row_mean(values)
    scale = lax.rsqrt(row_mean(centred * centred) + EPSILON)
    return centred * scale, scale


def norm_pull(normal, scale, cotangent):
    return scale * (cotangent - row_mean(cotangent) - normal * row_mean(cotangent * normal))


def others(axis, count):
    me = lax.axis_index(axis)
    return [{axis: lax.rem(me + step, count)} for step in range(1, count)]


def remote(src, dst, send_sem, recv_sem, peer):
    copy = pltpu.make_async_remote_copy(
        src_ref=src,
        dst_ref=dst,
        send_sem=send_sem,
        recv_sem=recv_sem,
        device_id=peer,
        device_id_type=MESH_ID,
    )
    copy.start()
    return copy


def spans_of(total, step):
    return [(at, min(step, total - at)) for at in range(0, total, step)]


def col_sum(values):
    return jnp.sum(values, axis=0, keepdims=True)


def main_kernel(
    shards,
    replicas,
    grad_scale,
    tokens_hbm,
    offsets_hbm,
    owners_hbm,
    grad_hbm,
    layer_hbm,
    input_hbm,
    pre_gain_hbm,
    pre_bias_hbm,
    up_hbm,
    unit_bias_hbm,
    down_hbm,
    post_gain_hbm,
    post_bias_hbm,
    merge_hbm,
    act_ref,
    norm_ref,
    unit_ref,
    tokens_ref,
    offsets_ref,
    owners_ref,
    grad_ref,
    layer_ref,
    input_ref,
    pre_gain_ref,
    pre_bias_ref,
    up_ref,
    unit_bias_ref,
    down_ref,
    post_gain_ref,
    post_bias_ref,
    merge_ref,
    send_buf,
    recv_buf,
    normed,
    normals,
    scales,
    head_normal,
    head_unit,
    head_scale,
    head_rms,
    slopes,
    res_keep,
    res_out,
    res_in,
    hidden,
    part_keep,
    part_out,
    part_in,
    head_seq,
    head_dp,
    head_last,
    unit_seq,
    unit_dp,
    unit_last,
    late_seq,
    late_dp,
    late_last,
    load_sem,
    seq_send,
    seq_recv,
    enc_send,
    enc_recv,
    sum_send,
    sum_recv,
):
    me = lax.axis_index("seq")
    replica = lax.axis_index("dp")
    core = lax.axis_index("enc")
    other = 1 - core
    partner = {"enc": other}
    seq_peers = others("seq", shards)
    dp_peers = others("dp", replicas)
    peers = [partner] + seq_peers + dp_peers
    barrier = pltpu.get_barrier_semaphore()
    for peer in peers:
        pl.semaphore_signal(barrier, inc=1, device_id=peer, device_id_type=MESH_ID)

    blocks, tiles, own, width = layer_hbm.shape
    rows = blocks * SUB
    slots = blocks * tiles
    wide = res_out.shape[0]
    units = up_hbm.shape[0]
    unit_pad = up_ref.shape[0]
    rows_dev = grad_hbm.shape[0] // own
    images = tokens_hbm.shape[1]
    window = own * WINDOW
    places = shards * window
    chunks = spans_of(units, CHUNK)

    started = []

    def load(src, dst):
        copy = pltpu.make_async_copy(src, dst, load_sem.at[len(started)])
        copy.start()
        started.append(copy)
        return copy

    table_loads = [
        load(tokens_hbm, tokens_ref),
        load(offsets_hbm, offsets_ref),
        load(owners_hbm, owners_ref),
    ]
    grad_load = load(grad_hbm, grad_ref)
    input_loads = [
        [
            load(
                input_hbm.at[:, tile, pl.ds(half * own, own), :],
                input_ref.at[half, :, pl.ds(tile * own, own), :],
            )
            for tile in range(tiles)
        ]
        for half in range(2)
    ]
    pre_loads = [load(pre_gain_hbm, pre_gain_ref), load(pre_bias_hbm, pre_bias_ref)]
    bias_load = load(unit_bias_hbm, unit_bias_ref)
    up_loads = [load(up_hbm.at[pl.ds(at, size)], up_ref.at[pl.ds(at, size)]) for at, size in chunks]
    layer_loads = [
        load(layer_hbm.at[:, tile], layer_ref.at[:, pl.ds(tile * own, own), :]) for tile in range(tiles)
    ]
    post_loads = [
        load(post_gain_hbm, post_gain_ref),
        load(post_bias_hbm, post_bias_ref),
        load(merge_hbm, merge_ref),
    ]
    down_loads = [
        load(down_hbm.at[pl.ds(at, size)], down_ref.at[pl.ds(at, size)]) for at, size in chunks
    ]

    if unit_pad > units:
        up_ref[units:unit_pad, :] = jnp.zeros((unit_pad - units, width), BF16)
        hidden[:, :, units:unit_pad] = jnp.zeros((2, wide, unit_pad - units), BF16)
    if wide > rows:
        normed[:, rows:wide, :] = jnp.zeros((2, wide - rows, width), BF16)
        res_out[rows:wide, :] = jnp.zeros((wide - rows, width), BF16)

    for copy in table_loads:
        copy.wait()
    place = lax.broadcasted_iota(jnp.int32, (places, own * rows_dev), 0)
    chip, step = place // window, place % WINDOW
    patch = (place // WINDOW) % own
    source = jnp.full((places, own * rows_dev), -own * rows_dev, jnp.int32)
    for image in range(images):
        taken = (chip == owners_ref[me, image]) & (step < tokens_ref[me, image])
        source = jnp.where(taken, offsets_ref[me, image] + step, source)
    column = lax.broadcasted_iota(jnp.int32, (places, own * rows_dev), 1)
    pack = jnp.where(column == source + patch * rows_dev, 1.0, 0.0).astype(BF16)
    grad_load.wait()
    packed = jnp.dot(pack, grad_ref[...], preferred_element_type=F32)
    send_buf[...] = packed.astype(BF16).reshape(shards, window, width)
    pl.semaphore_wait(barrier, len(peers))
    token_copies = [
        remote(
            send_buf.at[peer["seq"]], recv_buf.at[me], seq_send.at[index], seq_recv.at[index], peer
        )
        for index, peer in enumerate(seq_peers)
    ]
    recv_buf[me] = send_buf[me]

    for copy in pre_loads:
        copy.wait()
    pre_gain = pre_gain_ref[...].reshape(1, -1)
    pre_bias = pre_bias_ref[...].reshape(1, -1)
    for half in range(2):
        for copy in input_loads[half]:
            copy.wait()
        for block in range(blocks):
            normal, scale = norm_parts(input_ref[half, block].astype(F32))
            normals[half, block] = normal
            scales[half, block] = jnp.broadcast_to(scale, (SUB, LANES))
            normed[half, block * SUB : (block + 1) * SUB, :] = (normal * pre_gain + pre_bias).astype(BF16)

    for copy in layer_loads + post_loads:
        copy.wait()
    post_gain = post_gain_ref[...].reshape(1, -1)
    post_bias = post_bias_ref[...].reshape(1, -1)
    merge_gain = merge_ref[...].reshape(1, -1)
    for block in range(blocks):
        normal, scale = norm_parts(layer_ref[block].astype(F32))
        affine = normal * post_gain + post_bias
        rms = lax.rsqrt(row_mean(affine * affine) + EPSILON)
        head_normal[block] = normal
        head_unit[block] = affine * rms
        head_scale[block] = jnp.broadcast_to(scale, (SUB, LANES))
        head_rms[block] = jnp.broadcast_to(rms, (SUB, LANES))

    place = lax.broadcasted_iota(jnp.int32, (rows, places), 1)
    chip, step = place // window, place % WINDOW
    patch = (place // WINDOW) % own
    target = jnp.full((rows, places), -1, jnp.int32)
    first = jnp.int32(0)
    for shard in range(shards):
        count = jnp.int32(0)
        for image in range(images):
            count += jnp.where(owners_ref[shard, image] == me, tokens_ref[shard, image], 0)
        target = jnp.where((chip == shard) & (step < count), (first + step) * own + patch, target)
        first += count
    row = lax.broadcasted_iota(jnp.int32, (rows, places), 0)
    unpack = jnp.where(row == target, 1.0, 0.0).astype(BF16)

    bias_load.wait()
    unit_bias = unit_bias_ref[...].reshape(1, -1)
    for (at, size), copy in zip(chunks, up_loads):
        copy.wait()
        for half in range(2):
            pre_act = lax.dot_general(
                normed[half], up_ref[at : at + size, :], NT, preferred_element_type=F32
            )
            slopes[half, :, at : at + size] = gelu_slope(pre_act + unit_bias[:, at : at + size])

    for copy in token_copies:
        copy.wait()
    landed = recv_buf[...].reshape(places, width)
    incoming_all = jnp.dot(unpack, landed, preferred_element_type=F32)
    totals = None
    for block in range(blocks):
        incoming = incoming_all[block * SUB : (block + 1) * SUB, :]
        normal = head_normal[block]
        unit = head_unit[block]
        scale = head_scale[block][:, 0:1]
        rms = head_rms[block][:, 0:1]
        unit_grad = incoming * merge_gain
        affine_grad = rms * (unit_grad - unit * row_mean(unit_grad * unit))
        res = norm_pull(normal, scale, affine_grad * post_gain)
        res_keep[block] = res
        res_out[block * SUB : (block + 1) * SUB, :] = res.astype(BF16)
        parts = [incoming * unit, affine_grad * normal, affine_grad, res]
        totals = parts if totals is None else [a + b for a, b in zip(totals, parts)]
    res_copy = remote(res_out, res_in, enc_send.at[0], enc_recv.at[0], partner)
    for index, total in enumerate(totals):
        head_seq[me, index : index + 1, :] = col_sum(total)

    sums = []

    def gather(buffer, place, axis_peers):
        copies = [
            remote(
                buffer.at[place],
                buffer.at[place],
                sum_send.at[len(sums) + index],
                sum_recv.at[len(sums) + index],
                peer,
            )
            for index, peer in enumerate(axis_peers)
        ]
        sums.extend(copies)
        return copies

    def settle(copies, buffer, count):
        for copy in copies:
            copy.wait()
        total = buffer[0]
        for index in range(1, count):
            total = total + buffer[index]
        return total

    head_copies = gather(head_seq, me, seq_peers)

    unit_rows = spans_of(units, width)
    unit_sums = []

    def down_half(half, res):
        for index, (at, size) in enumerate(chunks):
            if len(unit_sums) < len(chunks):
                down_loads[index].wait()
            back = lax.dot_general(res, down_ref[at : at + size, :], NT, preferred_element_type=F32)
            grads = back * slopes[half, :, at : at + size]
            hidden[half, :, at : at + size] = grads.astype(BF16)
            partial = col_sum(grads)
            if len(unit_sums) < len(chunks):
                unit_sums.append(partial)
            else:
                unit_sums[index] = unit_sums[index] + partial

    down_half(core, res_out[...])
    res_copy.wait()
    down_half(other, res_in[...])
    unit_seq[me] = jnp.zeros(unit_seq.shape[1:], F32)
    unit_total = jnp.concatenate(unit_sums, axis=1)
    for index, (at, size) in enumerate(unit_rows):
        unit_seq[me, index : index + 1, 0:size] = unit_total[:, at : at + size]
    unit_copies = gather(unit_seq, me, seq_peers)

    pieces = spans_of(width, width // PIECES)
    part_copies = []
    hidden_other = hidden[other]
    for index, (at, size) in enumerate(pieces):
        part = jnp.dot(hidden_other, up_ref[:, at : at + size], preferred_element_type=F32)
        part_keep[0, :, at : at + size] = part
        part_out[index] = part.astype(BF16)
        part_copies.append(
            remote(
                part_out.at[index],
                part_in.at[index],
                enc_send.at[1 + index],
                enc_recv.at[1 + index],
                partner,
            )
        )
    head_dp[replica] = settle(head_copies, head_seq, shards)
    head_copies = gather(head_dp, replica, dp_peers)
    hidden_own = hidden[core]
    for at, size in pieces:
        part_keep[1, :, at : at + size] = jnp.dot(
            hidden_own, up_ref[:, at : at + size], preferred_element_type=F32
        )
    totals = None
    for index, half in enumerate((other, core)):
        for block in range(blocks):
            part = part_keep[index, block * SUB : (block + 1) * SUB, :]
            parts = [part * normals[half, block], part]
            totals = parts if totals is None else [a + b for a, b in zip(totals, parts)]
    for index, total in enumerate(totals):
        late_seq[me, index : index + 1, :] = col_sum(total)
    late_copies = gather(late_seq, me, seq_peers)
    unit_dp[replica] = settle(unit_copies, unit_seq, shards)
    unit_copies = gather(unit_dp, replica, dp_peers)

    for copy in part_copies:
        copy.wait()
    for block in range(blocks):
        span = slice(block * SUB, (block + 1) * SUB)
        theirs = jnp.concatenate([part_in[index, span, :] for index in range(len(pieces))], axis=1)
        upstream = part_keep[1, span, :] + theirs.astype(F32)
        act = res_keep[block] + norm_pull(
            normals[core, block], scales[core, block][:, 0:1], upstream * pre_gain
        )
        act_ref[block] = act.astype(BF16)

    late_dp[replica] = settle(late_copies, late_seq, shards)
    late_copies = gather(late_dp, replica, dp_peers)
    head_last[core] = settle(head_copies, head_dp, replicas)
    unit_last[core] = settle(unit_copies, unit_dp, replicas) * grad_scale
    head_copies = gather(head_last, core, [partner])
    unit_copies = gather(unit_last, core, [partner])
    late_last[core] = settle(late_copies, late_dp, replicas)
    late_copies = gather(late_last, core, [partner])
    norm_ref[0:4, :] = settle(head_copies, head_last, 2) * grad_scale
    for copy in unit_copies:
        copy.wait()
    for half in range(2):
        for index, (at, size) in enumerate(unit_rows):
            unit_ref[half : half + 1, at : at + size] = unit_last[half, index : index + 1, 0:size]
    norm_ref[4:6, :] = settle(late_copies, late_last, 2) * grad_scale


def write_kernel(act_ref, norm_ref, unit_ref, act_hbm, norm_hbm, unit_hbm, flat, sems):
    tiles, own = act_hbm.shape[1:3]
    copies = [
        pltpu.make_async_copy(
            act_ref.at[:, pl.ds(tile * own, own), :], act_hbm.at[:, tile], sems.at[tile]
        )
        for tile in range(tiles)
    ]
    copies.append(pltpu.make_async_copy(norm_ref, norm_hbm, sems.at[tiles]))
    for copy in copies:
        copy.start()
    flat[...] = jnp.concatenate([unit_ref[0:1, :], unit_ref[1:2, :]], axis=1).reshape(-1)
    last = pltpu.make_async_copy(flat, unit_hbm, sems.at[tiles + 1])
    last.start()
    for copy in copies + [last]:
        copy.wait()


def round_up(value, step):
    return (value + step - 1) // step * step


def body(
    lm_grad,
    image_tokens,
    image_offset,
    image_owner,
    mlp_input,
    layer_output,
    pre_gain,
    pre_bias,
    fc1_weight,
    fc1_bias,
    fc2_weight,
    post_gain,
    post_bias,
    merge_gain,
):
    shards = lax.axis_size("seq")
    replicas = lax.axis_size("dp")
    cores = lax.axis_size("enc")
    own, rows_dev, width = lm_grad.shape[1:]
    group, slots = mlp_input.shape[1:3]
    images = image_tokens.shape[2]
    units = fc1_bias.shape[0]
    tiles = SUB // own
    blocks = slots // tiles
    rows = blocks * SUB
    wide = round_up(rows, 2 * SUB)
    unit_pad = round_up(units, LANES)
    unit_rows = round_up(units, width) // width
    chunk_count = len(spans_of(units, CHUNK))
    grad_scale = 1.0 / math.sqrt(group * rows_dev * shards * replicas)

    hbm = pl.BlockSpec(memory_space=pl.ANY)
    vmem = pl.BlockSpec(memory_space=pltpu.VMEM)
    dma = pltpu.SemaphoreType.DMA
    smem = pltpu.SMEM((shards, images), jnp.int32)
    piece = width // PIECES

    def main_call(*refs):
        main_kernel(shards, replicas, grad_scale, *refs)

    vector = pltpu.VMEM((width,), F32)
    sum_count = 3 * (shards - 1 + replicas - 1 + 1)
    act, norms, unit_sums = pl.pallas_call(
        main_call,
        out_shape=(
            jax.ShapeDtypeStruct((blocks, SUB, width), BF16),
            jax.ShapeDtypeStruct((6, width), F32),
            jax.ShapeDtypeStruct((cores, units), F32),
        ),
        in_specs=[hbm] * 14,
        out_specs=(vmem,) * 3,
        scratch_shapes=[
            smem,
            smem,
            smem,
            pltpu.VMEM((own * rows_dev, width), BF16),
            pltpu.VMEM((blocks, SUB, width), BF16),
            pltpu.VMEM((cores, blocks, SUB, width), BF16),
            vector,
            vector,
            pltpu.VMEM((unit_pad, width), BF16),
            pltpu.VMEM((units,), F32),
            pltpu.VMEM((unit_pad, width), BF16),
            vector,
            vector,
            vector,
            pltpu.VMEM((shards, own * WINDOW, width), BF16),
            pltpu.VMEM((shards, own * WINDOW, width), BF16),
            pltpu.VMEM((cores, wide, width), BF16),
            pltpu.VMEM((cores, blocks, SUB, width), F32),
            pltpu.VMEM((cores, blocks, SUB, LANES), F32),
            pltpu.VMEM((blocks, SUB, width), F32),
            pltpu.VMEM((blocks, SUB, width), F32),
            pltpu.VMEM((blocks, SUB, LANES), F32),
            pltpu.VMEM((blocks, SUB, LANES), F32),
            pltpu.VMEM((cores, wide, unit_pad), F32),
            pltpu.VMEM((blocks, SUB, width), F32),
            pltpu.VMEM((wide, width), BF16),
            pltpu.VMEM((wide, width), BF16),
            pltpu.VMEM((cores, wide, unit_pad), BF16),
            pltpu.VMEM((cores, wide, width), F32),
            pltpu.VMEM((PIECES, wide, piece), BF16),
            pltpu.VMEM((PIECES, wide, piece), BF16),
            pltpu.VMEM((shards, 4, width), F32),
            pltpu.VMEM((replicas, 4, width), F32),
            pltpu.VMEM((cores, 4, width), F32),
            pltpu.VMEM((shards, unit_rows, width), F32),
            pltpu.VMEM((replicas, unit_rows, width), F32),
            pltpu.VMEM((cores, unit_rows, width), F32),
            pltpu.VMEM((shards, 2, width), F32),
            pltpu.VMEM((replicas, 2, width), F32),
            pltpu.VMEM((cores, 2, width), F32),
            dma((10 + 3 * tiles + 2 * chunk_count,)),
            dma((shards - 1,)),
            dma((shards - 1,)),
            dma((1 + PIECES,)),
            dma((1 + PIECES,)),
            dma((sum_count,)),
            dma((sum_count,)),
        ],
        compiler_params=pltpu.CompilerParams(
            collective_id=0, has_side_effects=True, vmem_limit_bytes=48 * 1024 * 1024
        ),
        name="main",
    )(*[pltpu.with_memory_space_constraint(operand, pltpu.HBM) for operand in (
        image_tokens[0],
        image_offset[0],
        image_owner[0],
        lm_grad[0].reshape(own * rows_dev, width),
        layer_output[0].transpose(1, 0, 2).reshape(blocks, tiles, own, width),
        mlp_input[0].transpose(1, 0, 2).reshape(blocks, tiles, group, width),
        pre_gain,
        pre_bias,
        fc1_weight.T,
        fc1_bias,
        fc2_weight,
        post_gain,
        post_bias,
        merge_gain,
    )])

    act_grad, norm_grads, unit_grads = pl.pallas_call(
        write_kernel,
        out_shape=(
            jax.ShapeDtypeStruct((blocks, tiles, own, width), BF16),
            jax.ShapeDtypeStruct((6, width), F32),
            jax.ShapeDtypeStruct((cores * units,), F32),
        ),
        in_specs=[vmem] * 3,
        out_specs=(hbm,) * 3,
        scratch_shapes=[pltpu.VMEM((cores * units,), F32), dma((tiles + 2,))],
        compiler_params=pltpu.CompilerParams(vmem_limit_bytes=4 * 1024 * 1024),
        name="write",
    )(act, norms, unit_sums)
    act_grad = act_grad.reshape(slots, own, width).transpose(1, 0, 2)
    return (act_grad[None], norm_grads, unit_grads)


def solution(mesh):
    in_specs = (
        P("dp", "enc", "seq", None),
        P("dp", None, None),
        P("dp", None, None),
        P("dp", None, None),
        P("dp", None, "seq", None),
        P("dp", "enc", "seq", None),
        P(),
        P(),
        P(None, "enc"),
        P("enc"),
        P("enc", None),
        P(),
        P(),
        P(),
    )
    out_specs = (P("dp", "enc", "seq", None), P(), P())
    return jax.shard_map(body, mesh=mesh, in_specs=in_specs, out_specs=out_specs, check_vma=False)
```

time: 52.1 us -> 29.2 us (0.56); the launches traced: 51.3 us -> 29 us
  local copies, waits for them, and re-layouts: 14.8 us -> 0 us
  matrix products: 7.32 us -> 0 us
    unnamed x34 -> x0, local copies, waits for them, and re-layouts: 12.7 us -> none
    dot_general x3 -> x0, matrix products: 7.32 us -> none  [the longest x1 2.78 us: body(): lax.dot_general(hidden_grad.astype(BF16), fc1_weight, (((1,), (1,)), ((),...]
    reshape x1 -> x0, local copies, waits for them, and re-layouts: 1.41 us -> none  [body(): return (act_grad[None], norm_grads, unit_grads.reshape(-1))]
    broadcast_in_dim x1 -> x0, local copies, waits for them, and re-layouts: 0.61 us -> none  [body(): units = jnp.sum(hidden_grad, axis=0, keepdims=True)]
where the time goes in v1:
time: 29.2 us; the launch traced here: 29 us
  Pallas kernels  28.4 us (97%)
  between operations  0.64 us (2%)
    pallas_call x1, Pallas kernels, body(): pl.pallas_call(main_call, out_shape=(jax.ShapeDtypeStruct((blocks, SUB, w...  27.6 us
    pallas_call x1, Pallas kernels, body(): pl.pallas_call(write_kernel, out_shape=(jax.ShapeDtypeStruct((blocks, til...  0.77 us

profile of v1, /device:TPU:0, one launch (start us, length us, event | category | flops | bytes accessed | tf_op | source)
XLA Modules:
  0.0 29.0 jit_solution(4005027401094032650)
XLA Ops:
  0.6 27.6 %main.1 = (bf16[15,8,1152]{2,1,0:T(8,128)(2,1)S(1)}, f32[6,1152]{1,0:T(8,128)S(1)}, f32[2,2152]{1,0:T(2,128)S(1)}) custom-call(s32[4,4]{1,0:T(4,128)} %bitcast.24, s32[4,4]{1,0:T(4,128)} %bitcast.25, s32[4,4]{1,0:T(4,128)} %bitcast.26, bf16[96,1152]{1,0:T(8,128)(2,1)} %bitcast.23, bf16[15,4,2,1152]{3,2,1,0:T(2,128)(2,1)} %bitcast.22, ...), custom_call_target="tpu_custom_call" | custom-call | tf_op jit(solution)/shard_map/main/pallas_call | solution.py:485
  28.2 0.8 %write.1 = (bf16[15,4,2,1152]{3,2,1,0:T(2,128)(2,1)}, f32[6,1152]{1,0:T(8,128)}, f32[4304]{0:T(1024)}) custom-call(bf16[15,8,1152]{2,1,0:T(8,128)(2,1)S(1)} %get-tuple-element.9.act_ref, f32[6,1152]{1,0:T(8,128)S(1)} %get-tuple-element.10.norm_ref, f32[2,2152]{1,0:T(2,128)S(1)} %get-tuple-element.11.unit_ref), custom_call_target="tpu_custom_call" | custom-call | tf_op jit(solution)/shard_map/write/pallas_call | solution.py:564

commit v2 on v1

--- a/solution.py
+++ b/solution.py
@@ -10,8 +10,8 @@
 WINDOW = 16
 SUB = 8
 LANES = 128
-CHUNK = 512
-PIECES = 3
+CHUNK = 256
+PIECE = 512
 EPSILON = 1e-06
 SLOPE_K = math.sqrt(2.0 / math.pi)
 CUBIC = 0.044715
@@ -22,10 +22,9 @@
 
 
 def gelu_slope(pre_act):
-    square = pre_act * pre_act
-    tangent = jnp.tanh(pre_act * (SLOPE_K + (SLOPE_K * CUBIC) * square))
-    half = 0.5 + 0.5 * tangent
-    return half + half * (1.0 - tangent) * pre_act * (SLOPE_K + (3.0 * SLOPE_K * CUBIC) * square)
+    inner = pre_act * (SLOPE_K + (SLOPE_K * CUBIC) * (pre_act * pre_act))
+    half = 0.5 + 0.5 * jnp.tanh(inner)
+    return half * (1.0 + (1.0 - half) * (6.0 * inner - (4.0 * SLOPE_K) * pre_act))
 
 
 def row_mean(values):
@@ -58,6 +57,17 @@
     )
     copy.start()
     return copy
+
+
+def mesh_others(axis, count, cores):
+    me = lax.axis_index(axis)
+    core = lax.axis_index("enc")
+    return [
+        {axis: lax.rem(me + step, count), "enc": lax.rem(core + flip, cores)}
+        for step in range(count)
+        for flip in range(cores)
+        if step + flip > 0
+    ]
 
 
 def spans_of(total, step):
@@ -114,8 +124,7 @@
     head_rms,
     slopes,
     res_keep,
-    res_out,
-    res_in,
+    res_all,
     hidden,
     part_keep,
     part_out,
@@ -127,8 +136,8 @@
     unit_dp,
     unit_last,
     late_seq,
+    late_total,
     late_dp,
-    late_last,
     load_sem,
     seq_send,
     seq_recv,
@@ -136,6 +145,8 @@
     enc_recv,
     sum_send,
     sum_recv,
+    late_send,
+    late_recv,
 ):
     me = lax.axis_index("seq")
     replica = lax.axis_index("dp")
@@ -144,15 +155,17 @@
     partner = {"enc": other}
     seq_peers = others("seq", shards)
     dp_peers = others("dp", replicas)
-    peers = [partner] + seq_peers + dp_peers
+    seq_all = mesh_others("seq", shards, 2)
+    dp_all = mesh_others("dp", replicas, 2)
+    greeted = seq_all + [peer for index, peer in enumerate(dp_all) if index > 0]
     barrier = pltpu.get_barrier_semaphore()
-    for peer in peers:
+    for peer in greeted:
         pl.semaphore_signal(barrier, inc=1, device_id=peer, device_id_type=MESH_ID)
 
     blocks, tiles, own, width = layer_hbm.shape
     rows = blocks * SUB
     slots = blocks * tiles
-    wide = res_out.shape[0]
+    wide = res_all.shape[1]
     units = up_hbm.shape[0]
     unit_pad = up_ref.shape[0]
     rows_dev = grad_hbm.shape[0] // own
@@ -202,10 +215,10 @@
 
     if unit_pad > units:
         up_ref[units:unit_pad, :] = jnp.zeros((unit_pad - units, width), BF16)
-        hidden[:, :, units:unit_pad] = jnp.zeros((2, wide, unit_pad - units), BF16)
+        hidden[:, units:unit_pad] = jnp.zeros((2 * wide, unit_pad - units), BF16)
     if wide > rows:
         normed[:, rows:wide, :] = jnp.zeros((2, wide - rows, width), BF16)
-        res_out[rows:wide, :] = jnp.zeros((wide - rows, width), BF16)
+        res_all[core, rows:wide, :] = jnp.zeros((wide - rows, width), BF16)
 
     for copy in table_loads:
         copy.wait()
@@ -221,7 +234,7 @@
     grad_load.wait()
     packed = jnp.dot(pack, grad_ref[...], preferred_element_type=F32)
     send_buf[...] = packed.astype(BF16).reshape(shards, window, width)
-    pl.semaphore_wait(barrier, len(peers))
+    pl.semaphore_wait(barrier, len(greeted))
     token_copies = [
         remote(
             send_buf.at[peer["seq"]], recv_buf.at[me], seq_send.at[index], seq_recv.at[index], peer
@@ -273,13 +286,14 @@
 
     bias_load.wait()
     unit_bias = unit_bias_ref[...].reshape(1, -1)
-    for (at, size), copy in zip(chunks, up_loads):
-        copy.wait()
-        for half in range(2):
-            pre_act = lax.dot_general(
-                normed[half], up_ref[at : at + size, :], NT, preferred_element_type=F32
-            )
-            slopes[half, :, at : at + size] = gelu_slope(pre_act + unit_bias[:, at : at + size])
+    for copy in up_loads:
+        copy.wait()
+    normed_all = normed[...].reshape(2 * wide, width)
+    for at, size in chunks:
+        pre_act = lax.dot_general(
+            normed_all, up_ref[at : at + size, :], NT, preferred_element_type=F32
+        )
+        slopes[:, at : at + size] = gelu_slope(pre_act + unit_bias[:, at : at + size])
 
     for copy in token_copies:
         copy.wait()
@@ -296,10 +310,10 @@
         affine_grad = rms * (unit_grad - unit * row_mean(unit_grad * unit))
         res = norm_pull(normal, scale, affine_grad * post_gain)
         res_keep[block] = res
-        res_out[block * SUB : (block + 1) * SUB, :] = res.astype(BF16)
+        res_all[core, block * SUB : (block + 1) * SUB, :] = res.astype(BF16)
         parts = [incoming * unit, affine_grad * normal, affine_grad, res]
         totals = parts if totals is None else [a + b for a, b in zip(totals, parts)]
-    res_copy = remote(res_out, res_in, enc_send.at[0], enc_recv.at[0], partner)
+    res_copy = remote(res_all.at[core], res_all.at[core], enc_send.at[0], enc_recv.at[0], partner)
     for index, total in enumerate(totals):
         head_seq[me, index : index + 1, :] = col_sum(total)
 
@@ -331,61 +345,58 @@
 
     unit_rows = spans_of(units, width)
     unit_sums = []
-
-    def down_half(half, res):
-        for index, (at, size) in enumerate(chunks):
-            if len(unit_sums) < len(chunks):
-                down_loads[index].wait()
-            back = lax.dot_general(res, down_ref[at : at + size, :], NT, preferred_element_type=F32)
-            grads = back * slopes[half, :, at : at + size]
-            hidden[half, :, at : at + size] = grads.astype(BF16)
-            partial = col_sum(grads)
-            if len(unit_sums) < len(chunks):
-                unit_sums.append(partial)
-            else:
-                unit_sums[index] = unit_sums[index] + partial
-
-    down_half(core, res_out[...])
+    for copy in down_loads:
+        copy.wait()
     res_copy.wait()
-    down_half(other, res_in[...])
+    res_rows = res_all[...].reshape(2 * wide, width)
+    for at, size in chunks:
+        back = lax.dot_general(
+            res_rows, down_ref[at : at + size, :], NT, preferred_element_type=F32
+        )
+        grads = back * slopes[:, at : at + size]
+        hidden[:, at : at + size] = grads.astype(BF16)
+        unit_sums.append(col_sum(grads))
     unit_seq[me] = jnp.zeros(unit_seq.shape[1:], F32)
     unit_total = jnp.concatenate(unit_sums, axis=1)
     for index, (at, size) in enumerate(unit_rows):
         unit_seq[me, index : index + 1, 0:size] = unit_total[:, at : at + size]
     unit_copies = gather(unit_seq, me, seq_peers)
 
-    pieces = spans_of(width, width // PIECES)
+    pieces = spans_of(width, PIECE)
     part_copies = []
-    hidden_other = hidden[other]
+    hidden_all = hidden[...]
     for index, (at, size) in enumerate(pieces):
-        part = jnp.dot(hidden_other, up_ref[:, at : at + size], preferred_element_type=F32)
-        part_keep[0, :, at : at + size] = part
-        part_out[index] = part.astype(BF16)
+        span = slice(at, at + size)
+        part = jnp.dot(hidden_all, up_ref[:, span], preferred_element_type=F32)
+        part_keep[:, :, span] = part.reshape(2, wide, size)
+        part_out[:, span] = part_keep[other, :, span].astype(BF16)
         part_copies.append(
             remote(
-                part_out.at[index],
-                part_in.at[index],
+                part_out.at[:, pl.ds(at, size)],
+                part_in.at[:, pl.ds(at, size)],
                 enc_send.at[1 + index],
                 enc_recv.at[1 + index],
                 partner,
             )
         )
+        gain_sum = None
+        for half in range(2):
+            for block in range(blocks):
+                at_row = half * wide + block * SUB
+                block_part = part[at_row : at_row + SUB, :]
+                term = block_part * normals[half, block, :, span]
+                gain_sum = term if gain_sum is None else gain_sum + term
+                bias_sum = block_part if half + block == 0 else bias_sum + block_part
+        late_seq[me, core, 0:1, span] = col_sum(gain_sum)
+        late_seq[me, core, 1:2, span] = col_sum(bias_sum)
+    late_copies = [
+        remote(
+            late_seq.at[me, core], late_seq.at[me, core], late_send.at[index], late_recv.at[index], peer
+        )
+        for index, peer in enumerate(seq_all)
+    ]
     head_dp[replica] = settle(head_copies, head_seq, shards)
     head_copies = gather(head_dp, replica, dp_peers)
-    hidden_own = hidden[core]
-    for at, size in pieces:
-        part_keep[1, :, at : at + size] = jnp.dot(
-            hidden_own, up_ref[:, at : at + size], preferred_element_type=F32
-        )
-    totals = None
-    for index, half in enumerate((other, core)):
-        for block in range(blocks):
-            part = part_keep[index, block * SUB : (block + 1) * SUB, :]
-            parts = [part * normals[half, block], part]
-            totals = parts if totals is None else [a + b for a, b in zip(totals, parts)]
-    for index, total in enumerate(totals):
-        late_seq[me, index : index + 1, :] = col_sum(total)
-    late_copies = gather(late_seq, me, seq_peers)
     unit_dp[replica] = settle(unit_copies, unit_seq, shards)
     unit_copies = gather(unit_dp, replica, dp_peers)
 
@@ -393,28 +404,51 @@
         copy.wait()
     for block in range(blocks):
         span = slice(block * SUB, (block + 1) * SUB)
-        theirs = jnp.concatenate([part_in[index, span, :] for index in range(len(pieces))], axis=1)
-        upstream = part_keep[1, span, :] + theirs.astype(F32)
+        upstream = part_keep[core, span, :] + part_in[span, :].astype(F32)
         act = res_keep[block] + norm_pull(
             normals[core, block], scales[core, block][:, 0:1], upstream * pre_gain
         )
         act_ref[block] = act.astype(BF16)
 
-    late_dp[replica] = settle(late_copies, late_seq, shards)
-    late_copies = gather(late_dp, replica, dp_peers)
+    for copy in late_copies:
+        copy.wait()
+    total = None
+    for shard in range(shards):
+        for half in range(2):
+            term = late_seq[shard, half]
+            total = term if total is None else total + term
+    total = total * grad_scale
+    late_total[0] = total[0:1, :]
+    late_total[1] = total[1:2, :]
+    late_dp[replica, core] = late_total[core]
+    base = len(seq_all)
+    late_copies = [
+        remote(
+            late_total.at[core],
+            late_dp.at[replica, core],
+            late_send.at[base + index],
+            late_recv.at[base + index],
+            peer,
+        )
+        for index, peer in enumerate(dp_all)
+    ]
     head_last[core] = settle(head_copies, head_dp, replicas)
     unit_last[core] = settle(unit_copies, unit_dp, replicas) * grad_scale
     head_copies = gather(head_last, core, [partner])
     unit_copies = gather(unit_last, core, [partner])
-    late_last[core] = settle(late_copies, late_dp, replicas)
-    late_copies = gather(late_last, core, [partner])
     norm_ref[0:4, :] = settle(head_copies, head_last, 2) * grad_scale
     for copy in unit_copies:
         copy.wait()
     for half in range(2):
         for index, (at, size) in enumerate(unit_rows):
             unit_ref[half : half + 1, at : at + size] = unit_last[half, index : index + 1, 0:size]
-    norm_ref[4:6, :] = settle(late_copies, late_last, 2) * grad_scale
+    for copy in late_copies:
+        copy.wait()
+    for half in range(2):
+        total = late_dp[0, half]
+        for index in range(1, replicas):
+            total = total + late_dp[index, half]
+        norm_ref[4 + half : 5 + half, :] = total
 
 
 def write_kernel(act_ref, norm_ref, unit_ref, act_hbm, norm_hbm, unit_hbm, flat, sems):
@@ -475,13 +509,14 @@
     vmem = pl.BlockSpec(memory_space=pltpu.VMEM)
     dma = pltpu.SemaphoreType.DMA
     smem = pltpu.SMEM((shards, images), jnp.int32)
-    piece = width // PIECES
+    piece_count = len(spans_of(width, PIECE))
 
     def main_call(*refs):
         main_kernel(shards, replicas, grad_scale, *refs)
 
     vector = pltpu.VMEM((width,), F32)
-    sum_count = 3 * (shards - 1 + replicas - 1 + 1)
+    sum_count = 2 * (shards - 1 + replicas - 1 + 1)
+    late_count = cores * (shards + replicas) - 2
     act, norms, unit_sums = pl.pallas_call(
         main_call,
         out_shape=(
@@ -515,30 +550,31 @@
             pltpu.VMEM((blocks, SUB, width), F32),
             pltpu.VMEM((blocks, SUB, LANES), F32),
             pltpu.VMEM((blocks, SUB, LANES), F32),
-            pltpu.VMEM((cores, wide, unit_pad), F32),
+            pltpu.VMEM((cores * wide, unit_pad), F32),
             pltpu.VMEM((blocks, SUB, width), F32),
+            pltpu.VMEM((cores, wide, width), BF16),
+            pltpu.VMEM((cores * wide, unit_pad), BF16),
+            pltpu.VMEM((cores, wide, width), F32),
             pltpu.VMEM((wide, width), BF16),
             pltpu.VMEM((wide, width), BF16),
-            pltpu.VMEM((cores, wide, unit_pad), BF16),
-            pltpu.VMEM((cores, wide, width), F32),
-            pltpu.VMEM((PIECES, wide, piece), BF16),
-            pltpu.VMEM((PIECES, wide, piece), BF16),
             pltpu.VMEM((shards, 4, width), F32),
             pltpu.VMEM((replicas, 4, width), F32),
             pltpu.VMEM((cores, 4, width), F32),
             pltpu.VMEM((shards, unit_rows, width), F32),
             pltpu.VMEM((replicas, unit_rows, width), F32),
             pltpu.VMEM((cores, unit_rows, width), F32),
-            pltpu.VMEM((shards, 2, width), F32),
-            pltpu.VMEM((replicas, 2, width), F32),
-            pltpu.VMEM((cores, 2, width), F32),
+            pltpu.VMEM((shards, cores, 2, width), F32),
+            pltpu.VMEM((cores, 1, width), F32),
+            pltpu.VMEM((replicas, cores, 1, width), F32),
             dma((10 + 3 * tiles + 2 * chunk_count,)),
             dma((shards - 1,)),
             dma((shards - 1,)),
-            dma((1 + PIECES,)),
-            dma((1 + PIECES,)),
+            dma((1 + piece_count,)),
+            dma((1 + piece_count,)),
             dma((sum_count,)),
             dma((sum_count,)),
+            dma((late_count,)),
+            dma((late_count,)),
         ],
         compiler_params=pltpu.CompilerParams(
             collective_id=0, has_side_effects=True, vmem_limit_bytes=48 * 1024 * 1024

time: 29.2 us -> 26.6 us (0.911)
  Pallas kernels: 28.4 us -> 25.8 us
    pallas_call x1, Pallas kernels: 27.6 us -> 25 us  [body(): pl.pallas_call(main_call, out_shape=(jax.ShapeDtypeStruct((blocks, SUB, w...]
where the time goes in v2:
time: 26.6 us; the launch traced here: 26.4 us
  Pallas kernels  25.8 us (97%)
  between operations  0.64 us (2%)
    pallas_call x1, Pallas kernels, body(): pl.pallas_call(main_call, out_shape=(jax.ShapeDtypeStruct((blocks, SUB, w...  25 us
    pallas_call x1, Pallas kernels, body(): pl.pallas_call(write_kernel, out_shape=(jax.ShapeDtypeStruct((blocks, til...  0.77 us

profile of v2, /device:TPU:0, one launch (start us, length us, event | category | flops | bytes accessed | tf_op | source)
XLA Modules:
  0.0 26.4 jit_solution(15254640381923295201)
XLA Ops:
  0.6 25.0 %main.1 = (bf16[15,8,1152]{2,1,0:T(8,128)(2,1)S(1)}, f32[6,1152]{1,0:T(8,128)S(1)}, f32[2,2152]{1,0:T(2,128)S(1)}) custom-call(s32[4,4]{1,0:T(4,128)} %bitcast.24, s32[4,4]{1,0:T(4,128)} %bitcast.25, s32[4,4]{1,0:T(4,128)} %bitcast.26, bf16[96,1152]{1,0:T(8,128)(2,1)} %bitcast.23, bf16[15,4,2,1152]{3,2,1,0:T(2,128)(2,1)} %bitcast.22, ...), custom_call_target="tpu_custom_call" | custom-call | tf_op jit(solution)/shard_map/main/pallas_call | solution.py:520
  25.7 0.8 %write.1 = (bf16[15,4,2,1152]{3,2,1,0:T(2,128)(2,1)}, f32[6,1152]{1,0:T(8,128)}, f32[4304]{0:T(1024)}) custom-call(bf16[15,8,1152]{2,1,0:T(8,128)(2,1)S(1)} %get-tuple-element.9.act_ref, f32[6,1152]{1,0:T(8,128)S(1)} %get-tuple-element.10.norm_ref, f32[2,2152]{1,0:T(2,128)S(1)} %get-tuple-element.11.unit_ref), custom_call_target="tpu_custom_call" | custom-call | tf_op jit(solution)/shard_map/write/pallas_call | solution.py:600
